TPU v7x, 512 devices: a whole 4x8x8 slice. The times are simulated.
512 devices in a mesh: region: 32 (over x, y), shard: 16 (over z, core).
Axes of the slice: x: 4, y: 8, z: 8, core: 2. Of those that a mesh axis runs over, the one named last changes fastest.
Arguments:
- planes: bfloat16 [4, 16384, 512], P(None, ('region', 'shard')), may hold values from -6 to 6
- sed_weights: float32 [6, 4], replicated, may hold values from 0.1 to 2
- psf_taps: float32 [2, 6, 3, 25], replicated, may hold values from 0.004 to 0.08
- resample_rows: bfloat16 [16384, 128, 128], P(('region', 'shard')), may hold values from -0.5 to 0.5
- resample_cols: bfloat16 [16384, 128, 256], P(('region', 'shard')), may hold values from -0.375 to 0.375
- observed: bfloat16 [16384, 128, 128], P(('region', 'shard')), may hold values from -6 to 6
- exposure_meta: int32 [3, 16384], P(None, 'region'), may hold values from 0 to 15, as said below
- slot_counts: int32 [32, 16], P('region'), may hold values from 8 to 32, as said below
Outputs:
- plane_grad: float32 [4, 16384, 512], P(None, ('region', 'shard'))
Inputs may be any that keep to these rules, and one draw needn't show every extreme that they name: `exposure_meta`: row 0 is a row tile of the exposure's region, 0 to 15; row 1 a column tile, 0 to 1; row 2 a band, 0 to 5. `slot_counts`: the live slots of a device are its first ones. In every region one device has all 32 slots live, the others between 8 and 16.
All inputs are finite; a program needn't handle non-finite values.
Results may differ from a plain program's by a relative error of at most 0.003.
Values may be sent and summed in bfloat16 or wider, within the bound.
A program may use at most 64 MiB of HBM per device.

v0:
```python
import jax
import jax.numpy as jnp
from jax import lax
from jax.sharding import PartitionSpec as P

GROUP = 4


def passed_along(block, axis, distance):
    devices = range(lax.axis_size(axis))
    route = [(i - distance, i) for i in devices if i - distance in devices]
    return lax.ppermute(block, axis, route)


def band_tables(taps, width):
    tap_count = taps.shape[-1]
    offset = (
        jnp.arange(width, dtype=jnp.int32)[:, None]
        - jnp.arange(width, dtype=jnp.int32)[None, :]
        + tap_count // 2
    )
    selector = (offset[None, :, :] == jnp.arange(tap_count, dtype=jnp.int32)[:, None, None]).astype(
        jnp.float32
    )
    return jnp.einsum("btk,kij->btij", taps, selector, precision=lax.Precision.HIGHEST).astype(
        jnp.bfloat16
    )


def local(
    planes,
    sed_weights,
    psf_taps,
    resample_rows,
    resample_cols,
    observed,
    exposure_meta,
    slot_counts,
):
    shard_count = lax.axis_size("shard")
    my_index = lax.axis_index("shard")
    channel_count, tile_rows, col_total = planes.shape
    slot_count, out_rows, win_rows = resample_rows.shape
    win_cols = resample_cols.shape[2]
    region_rows = tile_rows * shard_count
    rim_rows = win_rows - tile_rows
    gathered = lax.all_gather(planes, "shard", axis=1, tiled=True)
    next_part = passed_along(gathered[:, :rim_rows], "region", -1)
    extended = jnp.concatenate([gathered, next_part], axis=1)
    rows_tab = band_tables(psf_taps[0], win_rows)
    cols_tab = band_tables(psf_taps[1], win_cols)
    live_counts = slot_counts[0]
    device_ids = jnp.arange(shard_count, dtype=jnp.int32)
    position = jnp.arange(slot_count, dtype=jnp.int32)
    my_count = jnp.sum(jnp.where(device_ids == my_index, live_counts, 0))
    row_maps, col_maps, pixel_sets = (resample_rows, resample_cols, observed)
    is_live = position < my_count
    region_slot = my_index * slot_count + position
    meta_total = exposure_meta.shape[1]
    matches = (jnp.arange(meta_total, dtype=jnp.int32)[:, None] == region_slot[None, :]).astype(
        jnp.int32
    )
    meta_sel = jnp.dot(exposure_meta, matches)
    live_rank = jnp.cumsum(is_live.astype(jnp.int32)) - 1
    picks = jnp.logical_and(is_live[:, None], live_rank[:, None] == position[None, :])
    live_order = jnp.sum(jnp.where(picks, position[:, None], 0), axis=0)
    live_total = jnp.sum(is_live.astype(jnp.int32))
    turn_total = (live_total + GROUP - 1) // GROUP

    def cut_window(start_row, start_col):
        return lax.dynamic_slice(
            extended, (jnp.int32(0), start_row, start_col), (channel_count, win_rows, win_cols)
        )

    def visit(turn_index, gradient):
        ranks = turn_index * GROUP + jnp.arange(GROUP, dtype=jnp.int32)
        usable = ranks < live_total
        chosen = jnp.take(live_order, jnp.minimum(ranks, slot_count - 1))
        row_start = jnp.take(meta_sel[0], chosen) * tile_rows
        col_start = jnp.take(meta_sel[1], chosen) * win_cols
        band_of = jnp.take(meta_sel[2], chosen)
        windows = jax.vmap(cut_window)(row_start, col_start)
        sed_sel = jnp.take(sed_weights, band_of, axis=0)
        py_mat = jnp.take(rows_tab, band_of, axis=0)
        px_mat = jnp.take(cols_tab, band_of, axis=0)
        ry_mat = jnp.take(row_maps, chosen, axis=0)
        rx_mat = jnp.take(col_maps, chosen, axis=0)
        pixels = jnp.take(pixel_sets, chosen, axis=0)
        mixed = jnp.sum(sed_sel[:, :, None, None] * windows.astype(jnp.float32), axis=1).astype(
            jnp.bfloat16
        )
        smeared = jnp.einsum(
            "gtiy,gyx->gtix", py_mat, mixed, preferred_element_type=jnp.float32
        ).astype(jnp.bfloat16)
        blurred = jnp.einsum(
            "gtix,gtjx->gij", smeared, px_mat, preferred_element_type=jnp.float32
        ).astype(jnp.bfloat16)
        sampled = jnp.einsum(
            "goy,gyx->gox", ry_mat, blurred, preferred_element_type=jnp.float32
        ).astype(jnp.bfloat16)
        model = jnp.einsum("gox,gpx->gop", sampled, rx_mat, preferred_element_type=jnp.float32)
        misfit = (model - pixels.astype(jnp.float32)).astype(jnp.bfloat16)
        back_rows = jnp.einsum(
            "goy,gop->gyp", ry_mat, misfit, preferred_element_type=jnp.float32
        ).astype(jnp.bfloat16)
        back = jnp.einsum(
            "gyp,gpx->gyx", back_rows, rx_mat, preferred_element_type=jnp.float32
        ).astype(jnp.bfloat16)
        unsmeared = jnp.einsum(
            "gtiy,gix->gtyx", py_mat, back, preferred_element_type=jnp.float32
        ).astype(jnp.bfloat16)
        window_grad = jnp.einsum(
            "gtyj,gtjx->gyx", unsmeared, px_mat, preferred_element_type=jnp.float32
        )
        contrib = sed_sel[:, :, None, None] * window_grad[:, None]
        for member in range(GROUP):
            corner = (jnp.int32(0), row_start[member], col_start[member])
            current = lax.dynamic_slice(gradient, corner, (channel_count, win_rows, win_cols))
            added = jnp.where(usable[member], contrib[member], 0.0)
            gradient = lax.dynamic_update_slice(gradient, current + added, corner)
        return gradient

    start = jnp.zeros((channel_count, region_rows + rim_rows, col_total), jnp.float32)
    gradient = lax.fori_loop(0, turn_total, visit, start)
    incoming = passed_along(gradient[:, region_rows:], "region", 1)
    own_rows = gradient[:, :region_rows].at[:, :rim_rows].add(incoming)
    return lax.psum_scatter(own_rows, "shard", scatter_dimension=1, tiled=True)


def solution(mesh):
    placed = (
        P(None, ("region", "shard"), None),
        P(),
        P(),
        P(("region", "shard"), None, None),
        P(("region", "shard"), None, None),
        P(("region", "shard"), None, None),
        P(None, "region"),
        P("region", None),
    )
    return jax.shard_map(
        local,
        mesh=mesh,
        in_specs=placed,
        out_specs=P(None, ("region", "shard"), None),
        check_vma=False,
    )
```

profile of v0, /device:TPU:2, one launch (start us, length us, event | category | flops | bytes accessed | tf_op | source)
XLA Modules:
  0.0 797.1 jit_solution(13557028132865648355)
XLA Ops:
  12.8 3.9 convert_bitcast_fusion
  16.7 40.7 %all-gather.2.cloned.1.call-done = bf16[4,512,512]{2,1,0:T(8,128)(2,1)} async-done(((bf16[4,32,512]{2,1,0:T(8,128)(2,1)}), bf16[4,512,512]{2,1,0:T(8,128)(2,1)}) %all-gather.2.cloned.1.call-update) | async-done | bytes 2097168 | tf_op jit(solution)/shard_map/all_gather | solution.py:47
  59.2 4.7 collective-permute-start
  66.0 2.1 copy.27
  68.1 2.0 copy.28
  70.4 2.5 collective-permute-done
  73.0 3.4 pad_maximum_fusion
  76.3 2.8 broadcast_in_dim.101
  79.2 311.7 %while.14 = (s32[]{:T(128)}, f32[4,608,512]{2,1,0:T(8,128)}, s32[]{:T(128)}, s32[3,32]{1,0:T(4,128)S(1)}, s32[32]{0:T(128)S(1)}, /*index=5*/s32[]{:T(128)}, f32[...) while((s32[]{:T(128)}, f32[4,608,512]{2,1,0:T(8,128)}, ...), condition=%wide.region_6.9_spmd, body=%wide.region_4.8_spmd.sunk | while | flops 728304896 | bytes 28457620 | solution.py:124
  104.1 2.2 gather_fusion.8
  106.9 12.7 %while.15 = (s32[]{:T(128)}, bf16[4,608,512]{2,1,0:T(8,128)(2,1)}, s32[4,3]{1,0:T(4,128)S(1)}, bf16[4,4,128,256]{3,2,1,0:T(8,128)(2,1)S(1)}, s32[]{:T(128)}) while((s32[]{:T(128)}, bf16[4,608,512]{2,1,0:T(8,128)(2,1)}, s32[4,3]{1,0:T(4,128)S(1)}, bf16[4,4,128,256]{3,2,1,0:T(8,128)(2,1)S(1)}, s32[]{:T(128)}) %tuple.81), condition=%wide.while_cond.1, body=%wide.while_body.1.sunk | while | flops 2 | bytes 524413 | solution.py:71
  107.6 2.5 bitcast_dynamic-update-slice_fusion.2
  110.8 2.5 bitcast_dynamic-update-slice_fusion.2
  114.0 2.5 bitcast_dynamic-update-slice_fusion.2
  117.1 2.5 bitcast_dynamic-update-slice_fusion.2
  119.9 2.3 gather_fusion.2
  129.5 5.3 dynamic_update_slice.16
  136.7 5.3 dynamic_update_slice.17
  143.8 5.2 dynamic_update_slice.18
  149.0 2.0 fusion.93
  151.0 5.2 dynamic_update_slice.19
  181.1 2.2 gather_fusion.8
  184.0 12.9 %while.15 = (s32[]{:T(128)}, bf16[4,608,512]{2,1,0:T(8,128)(2,1)}, s32[4,3]{1,0:T(4,128)S(1)}, bf16[4,4,128,256]{3,2,1,0:T(8,128)(2,1)S(1)}, s32[]{:T(128)}) while((s32[]{:T(128)}, bf16[4,608,512]{2,1,0:T(8,128)(2,1)}, s32[4,3]{1,0:T(4,128)S(1)}, bf16[4,4,128,256]{3,2,1,0:T(8,128)(2,1)S(1)}, s32[]{:T(128)}) %tuple.81), condition=%wide.while_cond.1, body=%wide.while_body.1.sunk | while | flops 2 | bytes 524413 | solution.py:71
  184.7 2.5 bitcast_dynamic-update-slice_fusion.2
  187.9 2.5 bitcast_dynamic-update-slice_fusion.2
  191.1 2.5 bitcast_dynamic-update-slice_fusion.2
  194.3 2.5 bitcast_dynamic-update-slice_fusion.2
  197.1 2.3 gather_fusion.2
  204.9 1.9 fusion.90
  206.8 5.9 dynamic_update_slice.16
  214.6 5.3 dynamic_update_slice.17
  219.9 1.9 fusion.92
  221.8 5.9 dynamic_update_slice.18
  227.7 2.1 fusion.93
  229.8 5.9 dynamic_update_slice.19
  260.6 2.2 gather_fusion.8
  263.4 12.9 %while.15 = (s32[]{:T(128)}, bf16[4,608,512]{2,1,0:T(8,128)(2,1)}, s32[4,3]{1,0:T(4,128)S(1)}, bf16[4,4,128,256]{3,2,1,0:T(8,128)(2,1)S(1)}, s32[]{:T(128)}) while((s32[]{:T(128)}, bf16[4,608,512]{2,1,0:T(8,128)(2,1)}, s32[4,3]{1,0:T(4,128)S(1)}, bf16[4,4,128,256]{3,2,1,0:T(8,128)(2,1)S(1)}, s32[]{:T(128)}) %tuple.81), condition=%wide.while_cond.1, body=%wide.while_body.1.sunk | while | flops 2 | bytes 524413 | solution.py:71
  264.1 2.5 bitcast_dynamic-update-slice_fusion.2
  267.4 2.5 bitcast_dynamic-update-slice_fusion.2
  270.6 2.5 bitcast_dynamic-update-slice_fusion.2
  273.7 2.5 bitcast_dynamic-update-slice_fusion.2
  276.6 2.3 gather_fusion.2
  286.3 5.9 dynamic_update_slice.16
  292.1 2.0 fusion.91
  294.1 5.9 dynamic_update_slice.17
  301.9 3.9 dynamic_update_slice.18
  305.8 2.1 fusion.93
  307.9 5.8 dynamic_update_slice.19
  338.6 2.2 gather_fusion.8
  341.4 12.7 %while.15 = (s32[]{:T(128)}, bf16[4,608,512]{2,1,0:T(8,128)(2,1)}, s32[4,3]{1,0:T(4,128)S(1)}, bf16[4,4,128,256]{3,2,1,0:T(8,128)(2,1)S(1)}, s32[]{:T(128)}) while((s32[]{:T(128)}, bf16[4,608,512]{2,1,0:T(8,128)(2,1)}, s32[4,3]{1,0:T(4,128)S(1)}, bf16[4,4,128,256]{3,2,1,0:T(8,128)(2,1)S(1)}, s32[]{:T(128)}) %tuple.81), condition=%wide.while_cond.1, body=%wide.while_body.1.sunk | while | flops 2 | bytes 524413 | solution.py:71
  342.2 2.5 bitcast_dynamic-update-slice_fusion.2
  345.3 2.5 bitcast_dynamic-update-slice_fusion.2
  348.5 2.5 bitcast_dynamic-update-slice_fusion.2
  351.7 2.5 bitcast_dynamic-update-slice_fusion.2
  354.5 2.3 gather_fusion.2
  364.1 5.3 dynamic_update_slice.16
  371.2 5.3 dynamic_update_slice.17
  378.3 5.3 dynamic_update_slice.18
  383.6 2.0 fusion.93
  385.6 5.3 dynamic_update_slice.19
  394.0 4.7 slice.100
  398.6 9.4 %collective-permute-done.1 = f32[4,96,512]{2,1,0:T(8,128)S(1)} collective-permute-done((f32[4,96,512]{2,1,0:T(8,128)S(1)}, f32[4,96,512]{2,1,0:T(8,128)S(1)}, u32[]{:S(2)}, u32[]{:S(2)}) %collective-permute-start.1) | collective-permute-done | bytes 786464 | tf_op jit(solution)/shard_map/ppermute | solution.py:12
  408.0 2.2 add_dynamic-update-slice_fusion
  410.3 380.0 %reduce-scatter.2.cloned.1.call-done = f32[4,32,512]{2,1,0:T(8,128)} async-done(((f32[4,512,512]{2,1,0:T(8,128)}), f32[4,32,512]{2,1,0:T(8,128)}) %reduce-scatter.2.cloned.1.call-update) | async-done | bytes 262160 | tf_op jit(solution)/shard_map/reduce_scatter | solution.py:127
  (196 shorter events, 104.7 us)
Async XLA Ops:
  6.5 63.7 %copy-start = (s32[3,512]{1,0:T(4,128)S(1)}, s32[3,512]{1,0:T(4,128)}, u32[]{:S(2)}) copy-start(s32[3,512]{1,0:T(4,128)} %param.22) | copy-start | bytes 18436
  6.5 50.8 %all-gather.2.cloned.1.call-start = ((), (), s32[]{:S(2)}) async-start(), calls=%async_computation.1 | async-start | bytes 2228224 | tf_op jit(solution)/shard_map/all_gather | solution.py:47
  7.3 783.0 %reduce-scatter.2.cloned.1.call-start = ((), (), s32[]{:S(2)}) async-start(), calls=%async_computation.2 | async-start | bytes 4456448 | tf_op jit(solution)/shard_map/reduce_scatter | solution.py:127
  12.8 53.1 %copy-start.3 = (f32[6,4]{0,1:T(4,128)S(1)}, f32[6,4]{0,1:T(4,128)}, u32[]{:S(2)}) copy-start(f32[6,4]{0,1:T(4,128)} %param.17) | copy-start | bytes 292
  59.2 13.8 %collective-permute-start = (bf16[4,96,512]{2,1,0:T(8,128)(2,1)}, bf16[4,96,512]{2,1,0:T(8,128)(2,1)}, u32[]{:S(2)}, u32[]{:S(2)}) collective-permute-start(bf16[4,96,512]{2,1,0:T(8,128)(2,1)} %slice.142), channel_id=1, source_target_pairs={{16,0},{32,16},{48,32},{64,48},{80,64},{96,80},{112,96},{128,112},... | collective-permute-start | bytes 1179656 | tf_op jit(solution)/shard_map/ppermute | solution.py:12
  76.3 2.8 copy-start.1
  106.9 15.4 %copy-start.2 = (bf16[4,3,128,128]{3,2,1,0:T(8,128)(2,1)}, bf16[4,3,128,128]{3,2,1,0:T(8,128)(2,1)S(1)}, u32[]{:S(2)}) copy-start(bf16[4,3,128,128]{3,2,1,0:T(8,128)(2,1)S(1)} %gather_fusion.6) | copy-start | bytes 1179652 | tf_op jit(solution)/shard_map/while
  183.9 15.5 %copy-start.2 = (bf16[4,3,128,128]{3,2,1,0:T(8,128)(2,1)}, bf16[4,3,128,128]{3,2,1,0:T(8,128)(2,1)S(1)}, u32[]{:S(2)}) copy-start(bf16[4,3,128,128]{3,2,1,0:T(8,128)(2,1)S(1)} %gather_fusion.6) | copy-start | bytes 1179652 | tf_op jit(solution)/shard_map/while
  263.4 15.5 %copy-start.2 = (bf16[4,3,128,128]{3,2,1,0:T(8,128)(2,1)}, bf16[4,3,128,128]{3,2,1,0:T(8,128)(2,1)S(1)}, u32[]{:S(2)}) copy-start(bf16[4,3,128,128]{3,2,1,0:T(8,128)(2,1)S(1)} %gather_fusion.6) | copy-start | bytes 1179652 | tf_op jit(solution)/shard_map/while
  341.4 15.4 %copy-start.2 = (bf16[4,3,128,128]{3,2,1,0:T(8,128)(2,1)}, bf16[4,3,128,128]{3,2,1,0:T(8,128)(2,1)S(1)}, u32[]{:S(2)}) copy-start(bf16[4,3,128,128]{3,2,1,0:T(8,128)(2,1)S(1)} %gather_fusion.6) | copy-start | bytes 1179652 | tf_op jit(solution)/shard_map/while
  392.0 16.0 %collective-permute-start.1 = (f32[4,96,512]{2,1,0:T(8,128)S(1)}, f32[4,96,512]{2,1,0:T(8,128)S(1)}, u32[]{:S(2)}, u32[]{:S(2)}) collective-permute-start(f32[4,96,512]{2,1,0:T(8,128)S(1)} %slice.102), channel_id=1, source_target_pairs={{0,16},{16,32},{32,48},{48,64},{64,80},{80,96},{96,112},{112,128},... | collective-permute-start | bytes 2359304 | tf_op jit(solution)/shard_map/ppermute | solution.py:12
Sparse Core Ops, SparseCore 0:
  9.5 47.8 all-gather.1
  410.4 379.8 reduce-scatter.1
where the time goes:
time: 809 us; the launch traced here: 797 us
  waiting for transfers between devices  433 us (54%)
  local copies, waits for them, and re-layouts  208 us (26%)
  loops' own time  61.7 us (8%)
  other arithmetic  46.3 us (6%)
  matrix products  26.5 us (3%)
  between operations  14.2 us (2%)
    reduce_scatter x1, waiting for transfers between devices, local(): return lax.psum_scatter(own_rows, 'shard', scatter_dimension=1, tiled=True)  380 us
    dynamic_update_slice x16, local copies, waits for them, and re-layouts, visit(): gradient = lax.dynamic_update_slice(gradient, current + added, corner)  86.5 us
    another operation x1, loops' own time, local(): gradient = lax.fori_loop(0, turn_total, visit, start)  61.2 us
    gather x48, local copies, waits for them, and re-layouts  50.8 us
    all_gather x1, waiting for transfers between devices, local(): gathered = lax.all_gather(planes, 'shard', axis=1, tiled=True)  40.7 us
    add x16, other arithmetic, visit(): gradient = lax.dynamic_update_slice(gradient, current + added, corner)  30.8 us
  transfers between devices with their start and end apart: 4, of which 4 were waited for; matrix products, arithmetic and copies ran while one was open for 2% of the time, Pallas kernels for 0%

commit v1 on v0

--- a/solution.py
+++ b/solution.py
@@ -44,7 +44,14 @@
     win_cols = resample_cols.shape[2]
     region_rows = tile_rows * shard_count
     rim_rows = win_rows - tile_rows
-    gathered = lax.all_gather(planes, "shard", axis=1, tiled=True)
+    ring = [planes]
+    for hop in range(15):
+        ring.append(lax.ppermute(ring[-1], "shard", [(dev, (dev + 1) % 16) for dev in range(16)]))
+    gathered = jnp.roll(
+        jnp.concatenate(ring[::-1], axis=1),
+        (lax.axis_index("shard") + 1) * ring[0].shape[1],
+        axis=1,
+    )
     next_part = passed_along(gathered[:, :rim_rows], "region", -1)
     extended = jnp.concatenate([gathered, next_part], axis=1)
     rows_tab = band_tables(psf_taps[0], win_rows)

time: 809 us -> 869 us (1.074)
  the two profiles are of different devices: /device:TPU:2 before, /device:TPU:10 now
where the time goes in v1:
time: 869 us; the launch traced here: 858 us
  waiting for transfers between devices  534 us (61%)
  local copies, waits for them, and re-layouts  199 us (23%)
  loops' own time  43.6 us (5%)
  other arithmetic  40 us (5%)
  matrix products  21.3 us (2%)
  between operations  14.3 us (2%)
    reduce_scatter x1, waiting for transfers between devices, local(): return lax.psum_scatter(own_rows, 'shard', scatter_dimension=1, tiled=True)  370 us
    ppermute x2, waiting for transfers between devices, passed_along(): return lax.ppermute(block, axis, route)  86.2 us
    ppermute x15, waiting for transfers between devices, local(): lax.ppermute(ring[-1], 'shard', [(dev, (dev + 1) % 16) for dev in range(1...  77.9 us
    dynamic_update_slice x12, local copies, waits for them, and re-layouts, visit(): gradient = lax.dynamic_update_slice(gradient, current + added, corner)  63 us
    another operation x1, loops' own time, local(): gradient = lax.fori_loop(0, turn_total, visit, start)  43.2 us
    unnamed x77, local copies, waits for them, and re-layouts  41.1 us
    gather x36, local copies, waits for them, and re-layouts  35.8 us
    add x12, other arithmetic, visit(): gradient = lax.dynamic_update_slice(gradient, current + added, corner)  23.2 us
  transfers between devices with their start and end apart: 18, of which 17 were waited for; matrix products, arithmetic and copies ran while one was open for 3% of the time, Pallas kernels for 0%

profile of v1, /device:TPU:10, one launch (start us, length us, event | category | flops | bytes accessed | tf_op | source)
XLA Modules:
  0.0 857.6 jit_solution(5440675356321508059)
XLA Ops:
  6.6 11.3 %collective-permute-done = bf16[4,32,512]{2,1,0:T(8,128)(2,1)S(1)} collective-permute-done((bf16[4,32,512]{2,1,0:T(8,128)(2,1)}, bf16[4,32,512]{2,1,0:T(8,128)(2,1)S(1)}, u32[]{:S(2)}, u32[]{:S(2)}) %collective-permute-start) | collective-permute-done | bytes 131104 | tf_op jit(solution)/shard_map/ppermute | solution.py:49
  17.9 5.6 collective-permute-done.1
  23.5 5.6 collective-permute-done.2
  29.8 5.6 collective-permute-done.3
  36.0 5.6 collective-permute-done.4
  42.3 5.6 collective-permute-done.5
  48.6 5.6 collective-permute-done.6
  54.9 5.6 collective-permute-done.7
  61.1 5.6 collective-permute-done.8
  67.4 5.6 collective-permute-done.9
  73.9 4.7 collective-permute-done.10
  78.6 3.9 convert_bitcast_fusion
  86.9 3.4 collective-permute-done.12
  93.7 2.4 collective-permute-done.13
  98.3 3.8 collective-permute-done.14
  141.0 2.3 collective-permute-start.15
  145.5 2.1 copy.27
  147.6 2.0 copy.28
  151.6 2.7 pad_maximum_fusion
  154.3 2.9 broadcast_in_dim.101
  157.1 226.5 %while.14 = (s32[]{:T(128)}, f32[4,608,512]{2,1,0:T(8,128)}, s32[]{:T(128)}, s32[3,32]{1,0:T(4,128)S(1)}, s32[32]{0:T(128)S(1)}, /*index=5*/s32[]{:T(128)}, f32[...) while((s32[]{:T(128)}, f32[4,608,512]{2,1,0:T(8,128)}, ...), condition=%wide.region_6.9_spmd, body=%wide.region_4.8_spmd.sunk | while | flops 728304896 | bytes 28457620 | solution.py:131
  180.9 2.2 gather_fusion.8
  183.8 12.0 %while.15 = (s32[]{:T(128)}, bf16[4,608,512]{2,1,0:T(8,128)(2,1)}, s32[4,3]{1,0:T(4,128)S(1)}, bf16[4,4,128,256]{3,2,1,0:T(8,128)(2,1)S(1)}, s32[]{:T(128)}) while((s32[]{:T(128)}, bf16[4,608,512]{2,1,0:T(8,128)(2,1)}, s32[4,3]{1,0:T(4,128)S(1)}, bf16[4,4,128,256]{3,2,1,0:T(8,128)(2,1)S(1)}, s32[]{:T(128)}) %tuple.81), condition=%wide.while_cond.1, body=%wide.while_body.1.sunk | while | flops 2 | bytes 524413 | solution.py:78
  184.4 2.3 bitcast_dynamic-update-slice_fusion.2
  187.4 2.3 bitcast_dynamic-update-slice_fusion.2
  190.4 2.3 bitcast_dynamic-update-slice_fusion.2
  193.4 2.3 bitcast_dynamic-update-slice_fusion.2
  196.1 2.3 gather_fusion.2
  203.8 2.0 fusion.90
  205.8 5.2 dynamic_update_slice.16
  212.9 3.9 dynamic_update_slice.17
  218.7 5.2 dynamic_update_slice.18
  225.8 5.2 dynamic_update_slice.19
  254.9 2.2 gather_fusion.8
  257.7 12.1 %while.15 = (s32[]{:T(128)}, bf16[4,608,512]{2,1,0:T(8,128)(2,1)}, s32[4,3]{1,0:T(4,128)S(1)}, bf16[4,4,128,256]{3,2,1,0:T(8,128)(2,1)S(1)}, s32[]{:T(128)}) while((s32[]{:T(128)}, bf16[4,608,512]{2,1,0:T(8,128)(2,1)}, s32[4,3]{1,0:T(4,128)S(1)}, bf16[4,4,128,256]{3,2,1,0:T(8,128)(2,1)S(1)}, s32[]{:T(128)}) %tuple.81), condition=%wide.while_cond.1, body=%wide.while_body.1.sunk | while | flops 2 | bytes 524413 | solution.py:78
  258.4 2.3 bitcast_dynamic-update-slice_fusion.2
  261.4 2.3 bitcast_dynamic-update-slice_fusion.2
  264.4 2.4 bitcast_dynamic-update-slice_fusion.2
  267.4 2.3 bitcast_dynamic-update-slice_fusion.2
  270.0 2.3 gather_fusion.2
  277.8 2.0 fusion.90
  279.8 5.3 dynamic_update_slice.16
  287.0 5.2 dynamic_update_slice.17
  292.2 1.9 fusion.92
  294.1 5.7 dynamic_update_slice.18
  301.7 5.2 dynamic_update_slice.19
  330.8 2.2 gather_fusion.8
  333.6 12.1 %while.15 = (s32[]{:T(128)}, bf16[4,608,512]{2,1,0:T(8,128)(2,1)}, s32[4,3]{1,0:T(4,128)S(1)}, bf16[4,4,128,256]{3,2,1,0:T(8,128)(2,1)S(1)}, s32[]{:T(128)}) while((s32[]{:T(128)}, bf16[4,608,512]{2,1,0:T(8,128)(2,1)}, s32[4,3]{1,0:T(4,128)S(1)}, bf16[4,4,128,256]{3,2,1,0:T(8,128)(2,1)S(1)}, s32[]{:T(128)}) %tuple.81), condition=%wide.while_cond.1, body=%wide.while_body.1.sunk | while | flops 2 | bytes 524413 | solution.py:78
  334.3 2.4 bitcast_dynamic-update-slice_fusion.2
  337.3 2.3 bitcast_dynamic-update-slice_fusion.2
  340.3 2.4 bitcast_dynamic-update-slice_fusion.2
  343.4 2.3 bitcast_dynamic-update-slice_fusion.2
  346.0 2.3 gather_fusion.2
  353.7 2.1 fusion.90
  355.8 5.9 dynamic_update_slice.16
  363.7 5.2 dynamic_update_slice.17
  368.9 1.9 fusion.92
  370.8 5.7 dynamic_update_slice.18
  378.4 5.2 dynamic_update_slice.19
  384.8 2.7 collective-permute-start.16
  387.5 4.7 slice.100
  392.2 86.2 %collective-permute-done.16 = f32[4,96,512]{2,1,0:T(8,128)S(1)} collective-permute-done((f32[4,96,512]{2,1,0:T(8,128)S(1)}, f32[4,96,512]{2,1,0:T(8,128)S(1)}, u32[]{:S(2)}, u32[]{:S(2)}) %collective-permute-start.16) | collective-permute-done | bytes 786464 | tf_op jit(solution)/shard_map/ppermute | solution.py:12
  478.3 2.2 add_dynamic-update-slice_fusion
  480.6 370.2 %reduce-scatter.2.cloned.1.call-done = f32[4,32,512]{2,1,0:T(8,128)} async-done(((f32[4,512,512]{2,1,0:T(8,128)}), f32[4,32,512]{2,1,0:T(8,128)}) %reduce-scatter.2.cloned.1.call-update) | async-done | bytes 262160 | tf_op jit(solution)/shard_map/reduce_scatter | solution.py:134
  (241 shorter events, 127.5 us)
Async XLA Ops:
  6.5 143.1 %copy-start = (s32[3,512]{1,0:T(4,128)S(1)}, s32[3,512]{1,0:T(4,128)}, u32[]{:S(2)}) copy-start(s32[3,512]{1,0:T(4,128)} %param.22) | copy-start | bytes 18436
  6.5 79.6 %copy-start.23 = (s32[1,16]{1,0:T(1,128)S(1)}, s32[1,16]{1,0:T(1,128)}, u32[]{:S(2)}) copy-start(s32[1,16]{1,0:T(1,128)} %param.23) | copy-start | bytes 196
  6.5 844.2 %reduce-scatter.2.cloned.1.call-start = ((), (), s32[]{:S(2)}) async-start(), calls=%async_computation.1 | async-start | bytes 4456448 | tf_op jit(solution)/shard_map/reduce_scatter | solution.py:134
  6.5 11.3 %collective-permute-start = (bf16[4,32,512]{2,1,0:T(8,128)(2,1)}, bf16[4,32,512]{2,1,0:T(8,128)(2,1)S(1)}, u32[]{:S(2)}, u32[]{:S(2)}) collective-permute-start(bf16[4,32,512]{2,1,0:T(8,128)(2,1)} %param.16), channel_id=1, source_target_pairs={{0,1},{1,2},{2,3},{3,4},{4,5},{5,6},{6,7},{7,8},{8,9},{9,10},{10,1... | collective-permute-start | bytes 393224 | tf_op jit(solution)/shard_map/ppermute | solution.py:49
  17.9 5.6 collective-permute-start.1
  23.5 5.6 collective-permute-start.2
  29.1 0.7 copy-start.4
  29.8 5.6 collective-permute-start.3
  35.4 0.7 copy-start.6
  36.0 5.6 collective-permute-start.4
  41.6 0.7 copy-start.8
  42.3 5.6 collective-permute-start.5
  47.9 0.7 copy-start.10
  48.6 5.6 collective-permute-start.6
  54.2 0.7 copy-start.12
  54.9 5.6 collective-permute-start.7
  60.5 0.7 copy-start.14
  61.1 5.6 collective-permute-start.8
  66.7 0.7 copy-start.16
  67.4 5.6 collective-permute-start.9
  73.0 5.6 copy-start.18
  73.0 5.6 collective-permute-start.10
  78.6 3.9 copy-start.20
  78.6 5.7 collective-permute-start.11
  78.6 45.5 %copy-start.3 = (bf16[4,32,512]{2,1,0:T(8,128)(2,1)S(1)}, bf16[4,32,512]{2,1,0:T(8,128)(2,1)}, u32[]{:S(2)}) copy-start(bf16[4,32,512]{2,1,0:T(8,128)(2,1)} %param.16) | copy-start | bytes 393220
  84.3 5.9 collective-permute-start.12
  90.2 5.9 collective-permute-start.13
  96.2 5.9 collective-permute-start.14
  97.4 33.7 %copy-start.21 = (bf16[4,32,512]{2,1,0:T(8,128)(2,1)S(1)}, bf16[4,32,512]{2,1,0:T(8,128)(2,1)}, u32[]{:S(2)}) copy-start(bf16[4,32,512]{2,1,0:T(8,128)(2,1)} %copy-done.20) | copy-start | bytes 393220
  97.4 34.3 %copy-start.19 = (bf16[4,32,512]{2,1,0:T(8,128)(2,1)S(1)}, bf16[4,32,512]{2,1,0:T(8,128)(2,1)}, u32[]{:S(2)}) copy-start(bf16[4,32,512]{2,1,0:T(8,128)(2,1)} %copy-done.18) | copy-start | bytes 393220
  97.4 35.0 %copy-start.17 = (bf16[4,32,512]{2,1,0:T(8,128)(2,1)S(1)}, bf16[4,32,512]{2,1,0:T(8,128)(2,1)}, u32[]{:S(2)}) copy-start(bf16[4,32,512]{2,1,0:T(8,128)(2,1)} %copy-done.16) | copy-start | bytes 393220
  97.4 35.7 %copy-start.15 = (bf16[4,32,512]{2,1,0:T(8,128)(2,1)S(1)}, bf16[4,32,512]{2,1,0:T(8,128)(2,1)}, u32[]{:S(2)}) copy-start(bf16[4,32,512]{2,1,0:T(8,128)(2,1)} %copy-done.14) | copy-start | bytes 393220
  97.4 36.3 %copy-start.13 = (bf16[4,32,512]{2,1,0:T(8,128)(2,1)S(1)}, bf16[4,32,512]{2,1,0:T(8,128)(2,1)}, u32[]{:S(2)}) copy-start(bf16[4,32,512]{2,1,0:T(8,128)(2,1)} %copy-done.12) | copy-start | bytes 393220
  97.4 37.0 %copy-start.11 = (bf16[4,32,512]{2,1,0:T(8,128)(2,1)S(1)}, bf16[4,32,512]{2,1,0:T(8,128)(2,1)}, u32[]{:S(2)}) copy-start(bf16[4,32,512]{2,1,0:T(8,128)(2,1)} %copy-done.10) | copy-start | bytes 393220
  97.4 37.7 %copy-start.9 = (bf16[4,32,512]{2,1,0:T(8,128)(2,1)S(1)}, bf16[4,32,512]{2,1,0:T(8,128)(2,1)}, u32[]{:S(2)}) copy-start(bf16[4,32,512]{2,1,0:T(8,128)(2,1)} %copy-done.8) | copy-start | bytes 393220
  97.4 38.3 %copy-start.7 = (bf16[4,32,512]{2,1,0:T(8,128)(2,1)S(1)}, bf16[4,32,512]{2,1,0:T(8,128)(2,1)}, u32[]{:S(2)}) copy-start(bf16[4,32,512]{2,1,0:T(8,128)(2,1)} %copy-done.6) | copy-start | bytes 393220
  97.4 39.0 %copy-start.5 = (bf16[4,32,512]{2,1,0:T(8,128)(2,1)S(1)}, bf16[4,32,512]{2,1,0:T(8,128)(2,1)}, u32[]{:S(2)}) copy-start(bf16[4,32,512]{2,1,0:T(8,128)(2,1)} %copy-done.4) | copy-start | bytes 393220
  106.8 38.6 %copy-start.22 = (f32[6,4]{0,1:T(4,128)S(1)}, f32[6,4]{0,1:T(4,128)}, u32[]{:S(2)}) copy-start(f32[6,4]{0,1:T(4,128)} %param.17) | copy-start | bytes 292
  141.0 10.6 %collective-permute-start.15 = (bf16[4,96,512]{2,1,0:T(8,128)(2,1)}, bf16[4,96,512]{2,1,0:T(8,128)(2,1)}, u32[]{:S(2)}, u32[]{:S(2)}) collective-permute-start(bf16[4,96,512]{2,1,0:T(8,128)(2,1)} %constant_dynamic-slice_fusion.2), channel_id=1, source_target_pairs={{16,0},{32,16},{48,32},{64,48},{80,64},{96,80},{112,96},{128,112},... | collective-permute-start | bytes 1179656 | tf_op jit(solution)/shard_map/ppermute | solution.py:12
  151.6 5.6 copy-start.1
  183.7 17.6 %copy-start.2 = (bf16[4,3,128,128]{3,2,1,0:T(8,128)(2,1)}, bf16[4,3,128,128]{3,2,1,0:T(8,128)(2,1)S(1)}, u32[]{:S(2)}) copy-start(bf16[4,3,128,128]{3,2,1,0:T(8,128)(2,1)S(1)} %gather_fusion.6) | copy-start | bytes 1179652 | tf_op jit(solution)/shard_map/while
  257.7 17.6 %copy-start.2 = (bf16[4,3,128,128]{3,2,1,0:T(8,128)(2,1)}, bf16[4,3,128,128]{3,2,1,0:T(8,128)(2,1)S(1)}, u32[]{:S(2)}) copy-start(bf16[4,3,128,128]{3,2,1,0:T(8,128)(2,1)S(1)} %gather_fusion.6) | copy-start | bytes 1179652 | tf_op jit(solution)/shard_map/while
  333.6 17.7 %copy-start.2 = (bf16[4,3,128,128]{3,2,1,0:T(8,128)(2,1)}, bf16[4,3,128,128]{3,2,1,0:T(8,128)(2,1)S(1)}, u32[]{:S(2)}) copy-start(bf16[4,3,128,128]{3,2,1,0:T(8,128)(2,1)S(1)} %gather_fusion.6) | copy-start | bytes 1179652 | tf_op jit(solution)/shard_map/while
  384.8 93.5 %collective-permute-start.16 = (f32[4,96,512]{2,1,0:T(8,128)S(1)}, f32[4,96,512]{2,1,0:T(8,128)S(1)}, u32[]{:S(2)}, u32[]{:S(2)}) collective-permute-start(f32[4,96,512]{2,1,0:T(8,128)S(1)} %slice.102), channel_id=1, source_target_pairs={{0,16},{16,32},{32,48},{48,64},{64,80},{80,96},{96,112},{112,128},... | collective-permute-start | bytes 2359304 | tf_op jit(solution)/shard_map/ppermute | solution.py:12
Sparse Core Ops, SparseCore 0:
  480.7 370.0 reduce-scatter.1
